TPU v7x, 32 devices: a whole 2x2x4 slice. The times are simulated.
32 devices in a mesh: dp: 16 (over z, x, core), tensor: 2 (over y).
Axes of the slice: x: 2, y: 2, z: 4, core: 2. Of those that a mesh axis runs over, the one named last changes fastest.
Arguments:
- inputs: bfloat16 [2048, 2048], P('dp'), may hold values from -6 to 6
- segments: int32 [2048], P('dp'), may hold values from 0 to 1, as said below
- positions: int32 [2048], P('dp'), may hold values from 0 to 1999, as said below
- w_query: bfloat16 [2048, 2048], P('dp', 'tensor')
- w_key: bfloat16 [2048, 512], P('dp', 'tensor')
- w_value: bfloat16 [2048, 512], P('dp', 'tensor'), may hold values from -0.125 to 0.125
- w_out: bfloat16 [2048, 2048], P('dp', 'tensor'), may hold values from -0.5 to 0.5
- w_gate: bfloat16 [2048, 8192], P('dp', 'tensor'), may hold values from -0.125 to 0.125
- w_up: bfloat16 [2048, 8192], P('dp', 'tensor'), may hold values from -0.125 to 0.125
- w_down: bfloat16 [2048, 8192], P('dp', 'tensor'), may hold values from -0.125 to 0.125
- attn_gain: bfloat16 [2048], P('dp'), may hold values from 0.5 to 1.5
- mlp_gain: bfloat16 [2048], P('dp'), may hold values from 0.5 to 1.5
- out_grad: bfloat16 [2048, 2048], P('dp'), may hold values from -6 to 6
Outputs:
- output: bfloat16 [2048, 2048], P('dp')
- input_grad: float32 [2048, 2048], P('dp')
- query_grad: float32 [2048, 2048], P('dp', 'tensor')
- key_grad: float32 [2048, 512], P('dp', 'tensor')
- value_grad: float32 [2048, 512], P('dp', 'tensor')
- out_proj_grad: float32 [2048, 2048], P('dp', 'tensor')
- gate_grad: float32 [2048, 8192], P('dp', 'tensor')
- up_grad: float32 [2048, 8192], P('dp', 'tensor')
- down_grad: float32 [2048, 8192], P('dp', 'tensor')
- attn_gain_grad: float32 [2048], P('dp')
- mlp_gain_grad: float32 [2048], P('dp')
Inputs may be any that keep to these rules, and one draw needn't show every extreme that they name: `segments`: within each sequence of 128 tokens segment numbers start at 0 and rise by one where a document begins; documents span 200 to 2000 tokens of the packed stream, so a sequence's first document may have begun in the sequence before it. `positions`: A token's position within its document: it rises by one from token to token of a document and is 0 where a document begins; at a sequence's first token it continues a document that began earlier.
All inputs are finite; a program needn't handle non-finite values.
Results may differ from a plain program's by a relative error of at most 0.019.
The roundings to bfloat16 on the way count: a program that leaves them out, or rounds other values in their place, can miss the bound.
Values may be sent and summed in bfloat16 or wider, within the bound.
No kernel may reach another device: no remote copies, remote signals or barrier semaphores. Data moves between devices by JAX's collectives and lax.ppermute only.
A program may use at most 256 MiB of HBM per device.

v0:
```python
import math
import jax
import jax.numpy as jnp
from jax import lax
from jax.sharding import PartitionSpec as P

HEADS = 32
KV_HEADS = 8
HEAD_DIM = 64
norm_eps = 1e-05
rope_base = 500000.0
masked_score = -1e30


def rope_freqs(head_dim):
    index = jnp.arange(head_dim // 2, dtype=jnp.float32)
    inverse = rope_base ** (-2.0 * index / head_dim)
    wavelen = 2.0 * math.pi / inverse
    smooth = (8192.0 / wavelen - 1.0) / 3.0
    scaled = (1.0 - smooth) * inverse / 32.0 + smooth * inverse
    return jnp.where(wavelen < 2048.0, inverse, jnp.where(wavelen > 8192.0, inverse / 32.0, scaled))


def rotate(values, cosine, sine):
    half = values.shape[-1] // 2
    first = values[..., :half]
    second = values[..., half:]
    return jnp.concatenate(
        [first * cosine - second * sine, second * cosine + first * sine], axis=-1
    )


def norm_parts(values):
    scale = lax.rsqrt(jnp.mean(values * values, axis=-1, keepdims=True) + norm_eps)
    return (values * scale, scale)


def norm_back(grad, unit, scale, gain):
    weighted = grad * gain
    return (
        scale * (weighted - unit * jnp.mean(weighted * unit, axis=-1, keepdims=True)),
        jnp.sum(grad * unit, axis=0),
    )


def dot_last(left, right):
    return lax.dot_general(
        left, right, (((1,), (1,)), ((), ())), preferred_element_type=jnp.float32
    )


def dot_first(left, right):
    return lax.dot_general(
        left, right, (((0,), (0,)), ((), ())), preferred_element_type=jnp.float32
    )


def on_device(
    inputs,
    segments,
    positions,
    w_query,
    w_key,
    w_value,
    w_out,
    w_gate,
    w_up,
    w_down,
    attn_gain,
    mlp_gain,
    out_grad,
):
    length = inputs.shape[0]
    group = HEADS // KV_HEADS
    factor = HEAD_DIM ** (-0.5)
    residual = inputs.astype(jnp.float32)
    angle = positions.astype(jnp.float32)[:, None] * rope_freqs(HEAD_DIM)[None, :]
    cosine = jnp.cos(angle)[:, None, :]
    sine = jnp.sin(angle)[:, None, :]
    order = jnp.arange(length)
    allowed = (segments[:, None] == segments[None, :]) & (order[:, None] >= order[None, :])
    query_full, key_full, value_full, out_full, gain_one = (
        lax.all_gather(w_query, "dp", axis=0, tiled=True),
        lax.all_gather(w_key, "dp", axis=0, tiled=True),
        lax.all_gather(w_value, "dp", axis=0, tiled=True),
        lax.all_gather(w_out, "dp", axis=0, tiled=True),
        lax.all_gather(attn_gain, "dp", axis=0, tiled=True),
    )
    gain_one = gain_one.astype(jnp.float32)
    unit_one, scale_one = norm_parts(residual)
    normed_one = (unit_one * gain_one).astype(jnp.bfloat16)
    query_rot = rotate(
        jnp.dot(normed_one, query_full, preferred_element_type=jnp.float32).reshape(
            length, -1, HEAD_DIM
        ),
        cosine,
        sine,
    ).astype(jnp.bfloat16)
    key_rot = rotate(
        jnp.dot(normed_one, key_full, preferred_element_type=jnp.float32).reshape(
            length, -1, HEAD_DIM
        ),
        cosine,
        sine,
    ).astype(jnp.bfloat16)
    value_heads = (
        jnp.dot(normed_one, value_full, preferred_element_type=jnp.float32)
        .astype(jnp.bfloat16)
        .reshape(length, -1, HEAD_DIM)
    )
    kv_local = key_rot.shape[1]
    query_group = query_rot.reshape(length, kv_local, group, HEAD_DIM)
    scores = jnp.where(
        allowed,
        jnp.einsum("qhgd,khd->hgqk", query_group, key_rot, preferred_element_type=jnp.float32)
        * factor,
        masked_score,
    )
    top = jnp.max(scores, axis=-1, keepdims=True)
    expo = jnp.exp(scores - top)
    total = jnp.sum(expo, axis=-1, keepdims=True)
    log_total = top + jnp.log(total)
    weights_low = (expo / total).astype(jnp.bfloat16)
    attended = (
        jnp.einsum("hgqk,khd->qhgd", weights_low, value_heads, preferred_element_type=jnp.float32)
        .astype(jnp.bfloat16)
        .reshape(length, -1)
    )
    attn_out = lax.psum(dot_last(attended, out_full), "tensor")
    middle = residual + attn_out
    gate_full, up_full, down_full, gain_two = (
        lax.all_gather(w_gate, "dp", axis=0, tiled=True),
        lax.all_gather(w_up, "dp", axis=0, tiled=True),
        lax.all_gather(w_down, "dp", axis=0, tiled=True),
        lax.all_gather(mlp_gain, "dp", axis=0, tiled=True),
    )
    gain_two = gain_two.astype(jnp.float32)
    unit_two, scale_two = norm_parts(middle)
    normed_two = (unit_two * gain_two).astype(jnp.bfloat16)
    gate = jnp.dot(normed_two, gate_full, preferred_element_type=jnp.float32)
    upward = jnp.dot(normed_two, up_full, preferred_element_type=jnp.float32)
    sigma = jax.nn.sigmoid(gate)
    active = (gate * sigma * upward).astype(jnp.bfloat16)
    mlp_out = lax.psum(dot_last(active, down_full).astype(jnp.bfloat16), "tensor").astype(
        jnp.float32
    )
    output = (middle + mlp_out).astype(jnp.bfloat16)
    gate_back, up_back, down_back, gain_back = (
        lax.all_gather(w_gate, "dp", axis=0, tiled=True),
        lax.all_gather(w_up, "dp", axis=0, tiled=True),
        lax.all_gather(w_down, "dp", axis=0, tiled=True),
        lax.all_gather(mlp_gain, "dp", axis=0, tiled=True),
    )
    gain_back = gain_back.astype(jnp.float32)
    down_grad = dot_first(out_grad, active)
    active_grad = jnp.dot(out_grad, down_back, preferred_element_type=jnp.float32)
    gate_delta = (active_grad * upward * sigma * (1.0 + gate * (1.0 - sigma))).astype(jnp.bfloat16)
    up_delta = (active_grad * gate * sigma).astype(jnp.bfloat16)
    gate_grad = dot_first(normed_two, gate_delta)
    up_grad = dot_first(normed_two, up_delta)
    normed_two_grad = lax.psum(
        dot_last(gate_delta, gate_back) + dot_last(up_delta, up_back), "tensor"
    )
    middle_part, mlp_gain_grad = norm_back(normed_two_grad, unit_two, scale_two, gain_back)
    middle_grad = out_grad.astype(jnp.float32) + middle_part
    query_back, key_back, value_back, out_back, gain_first = (
        lax.all_gather(w_query, "dp", axis=0, tiled=True),
        lax.all_gather(w_key, "dp", axis=0, tiled=True),
        lax.all_gather(w_value, "dp", axis=0, tiled=True),
        lax.all_gather(w_out, "dp", axis=0, tiled=True),
        lax.all_gather(attn_gain, "dp", axis=0, tiled=True),
    )
    gain_first = gain_first.astype(jnp.float32)
    attn_delta = middle_grad.astype(jnp.bfloat16)
    out_proj_grad = dot_first(attn_delta, attended)
    head_delta = (
        jnp.dot(attn_delta, out_back, preferred_element_type=jnp.float32)
        .astype(jnp.bfloat16)
        .reshape(length, kv_local, group, HEAD_DIM)
    )
    rescored = jnp.where(
        allowed,
        jnp.einsum("qhgd,khd->hgqk", query_group, key_rot, preferred_element_type=jnp.float32)
        * factor,
        masked_score,
    )
    probs = jnp.exp(rescored - log_total)
    prob_grad = jnp.einsum(
        "qhgd,khd->hgqk", head_delta, value_heads, preferred_element_type=jnp.float32
    )
    row_total = jnp.sum(probs * prob_grad, axis=-1, keepdims=True)
    score_delta = (probs * (prob_grad - row_total)).astype(jnp.bfloat16)
    query_rot_grad = (
        jnp.einsum("hgqk,khd->qhgd", score_delta, key_rot, preferred_element_type=jnp.float32)
        * factor
    )
    key_rot_grad = (
        jnp.einsum("hgqk,qhgd->khd", score_delta, query_group, preferred_element_type=jnp.float32)
        * factor
    )
    value_delta = (
        jnp.einsum(
            "hgqk,qhgd->khd",
            probs.astype(jnp.bfloat16),
            head_delta,
            preferred_element_type=jnp.float32,
        )
        .astype(jnp.bfloat16)
        .reshape(length, -1)
    )
    query_delta = (
        rotate(query_rot_grad.reshape(length, -1, HEAD_DIM), cosine, -sine)
        .astype(jnp.bfloat16)
        .reshape(length, -1)
    )
    key_delta = rotate(key_rot_grad, cosine, -sine).astype(jnp.bfloat16).reshape(length, -1)
    query_grad = dot_first(normed_one, query_delta)
    key_grad = dot_first(normed_one, key_delta)
    value_grad = dot_first(normed_one, value_delta)
    local_first = (
        dot_last(query_delta, query_back)
        + dot_last(key_delta, key_back)
        + dot_last(value_delta, value_back)
    )
    normed_one_grad = lax.psum(local_first.astype(jnp.bfloat16), "tensor").astype(jnp.float32)
    input_part, attn_gain_grad = norm_back(normed_one_grad, unit_one, scale_one, gain_first)
    input_grad = middle_grad + input_part
    (
        query_grad,
        key_grad,
        value_grad,
        out_proj_grad,
        gate_grad,
        up_grad,
        down_grad,
        attn_gain_grad,
        mlp_gain_grad,
    ) = (
        lax.psum_scatter(query_grad, "dp", scatter_dimension=0, tiled=True),
        lax.psum_scatter(key_grad, "dp", scatter_dimension=0, tiled=True),
        lax.psum_scatter(value_grad, "dp", scatter_dimension=0, tiled=True),
        lax.psum_scatter(out_proj_grad, "dp", scatter_dimension=0, tiled=True),
        lax.psum_scatter(gate_grad, "dp", scatter_dimension=0, tiled=True),
        lax.psum_scatter(up_grad, "dp", scatter_dimension=0, tiled=True),
        lax.psum_scatter(down_grad, "dp", scatter_dimension=0, tiled=True),
        lax.psum_scatter(attn_gain_grad, "dp", scatter_dimension=0, tiled=True),
        lax.psum_scatter(mlp_gain_grad, "dp", scatter_dimension=0, tiled=True),
    )
    return (
        output,
        input_grad,
        query_grad,
        key_grad,
        value_grad,
        out_proj_grad,
        gate_grad,
        up_grad,
        down_grad,
        attn_gain_grad,
        mlp_gain_grad,
    )


def solution(mesh):
    in_specs = (
        P("dp", None),
        P("dp"),
        P("dp"),
        P("dp", "tensor"),
        P("dp", "tensor"),
        P("dp", "tensor"),
        P("dp", "tensor"),
        P("dp", "tensor"),
        P("dp", "tensor"),
        P("dp", "tensor"),
        P("dp"),
        P("dp"),
        P("dp", None),
    )
    out_specs = (
        P("dp", None),
        P("dp", None),
        P("dp", "tensor"),
        P("dp", "tensor"),
        P("dp", "tensor"),
        P("dp", "tensor"),
        P("dp", "tensor"),
        P("dp", "tensor"),
        P("dp", "tensor"),
        P("dp"),
        P("dp"),
    )
    return jax.shard_map(
        on_device, mesh=mesh, in_specs=in_specs, out_specs=out_specs, check_vma=False
    )
```

profile of v0, /device:TPU:0, one launch (start us, length us, event | category | flops | bytes accessed | tf_op | source)
XLA Modules:
  0.0 2104.6 jit_solution(7362402371754869214)
XLA Ops:
  10.7 23.3 %all-gather = bf16[16,1,128]{2,1,0:T(2,128)(2,1)S(1)} all-gather(bf16[1,1,128]{2,1,0:T(2,128)(2,1)} %bitcast.134), channel_id=1, replica_groups=mesh['dp'=16,'tensor'=2] {'dp'}, dimensions={0}, use_global_device_ids=true | all-gather | bytes 4352 | tf_op jit(solution)/shard_map/all_gather | solution.py:87
  34.0 1.2 fusion.17
  36.2 14.6 all-gather.10.cloned.1.call-done
  50.8 1.7 convolution_convert_fusion.3
  52.6 37.1 %all-gather.12.cloned.1.call-done = bf16[2048,256]{1,0:T(8,128)(2,1)} async-done(((bf16[128,256]{1,0:T(8,128)(2,1)}), bf16[2048,256]{1,0:T(8,128)(2,1)}) %all-gather.12.cloned.1.call-update) | async-done | bytes 1048592 | tf_op jit(solution)/shard_map/all_gather | solution.py:84
  89.8 2.0 fusion.38
  91.8 49.5 %all-gather.14.cloned.1.call-done = bf16[2048,1024]{1,0:T(8,128)(2,1)} async-done(((bf16[128,1024]{1,0:T(8,128)(2,1)}), bf16[2048,1024]{1,0:T(8,128)(2,1)}) %all-gather.14.cloned.1.call-update) | async-done | bytes 4194320 | tf_op jit(solution)/shard_map/all_gather | solution.py:83
  141.3 4.0 fusion.36
  147.0 45.3 %all-gather.16.cloned.1.call-done = bf16[2048,1024]{1,0:T(8,128)(2,1)} async-done(((bf16[128,1024]{1,0:T(8,128)(2,1)}), bf16[2048,1024]{1,0:T(8,128)(2,1)}) %all-gather.16.cloned.1.call-update) | async-done | bytes 4194320 | tf_op jit(solution)/shard_map/all_gather | solution.py:86
  192.3 4.7 fusion.42
  199.1 19.5 all-gather.1
  218.6 17.2 all-reduce.8.cloned.1.call-done
  235.8 1.4 multiply_reduce_fusion.3
  237.4 126.8 %all-gather.20.cloned.1.call-done = bf16[2048,4096]{1,0:T(8,128)(2,1)} async-done(((bf16[128,4096]{1,0:T(8,128)(2,1)}), bf16[2048,4096]{1,0:T(8,128)(2,1)}) %all-gather.20.cloned.1.call-update) | async-done | bytes 16777232 | tf_op jit(solution)/shard_map/all_gather | solution.py:133
  364.3 9.4 fusion.44
  373.7 117.4 %all-gather.18.cloned.1.call-done = bf16[2048,4096]{1,0:T(8,128)(2,1)} async-done(((bf16[128,4096]{1,0:T(8,128)(2,1)}), bf16[2048,4096]{1,0:T(8,128)(2,1)}) %all-gather.18.cloned.1.call-update) | async-done | bytes 16777232 | tf_op jit(solution)/shard_map/all_gather | solution.py:132
  491.1 9.4 fusion.43
  500.5 117.4 %all-gather.22.cloned.1.call-done = bf16[2048,4096]{1,0:T(8,128)(2,1)} async-done(((bf16[128,4096]{1,0:T(8,128)(2,1)}), bf16[2048,4096]{1,0:T(8,128)(2,1)}) %all-gather.22.cloned.1.call-update) | async-done | bytes 16777232 | tf_op jit(solution)/shard_map/all_gather | solution.py:134
  617.9 11.9 multiply_convert_fusion
  629.8 13.2 fusion.45
  643.0 12.9 convolution_add_fusion.1
  656.0 12.5 convolution_convert_fusion
  668.6 25.8 %all-reduce.10.cloned.1.call-done = f32[128,2048]{1,0:T(8,128)} async-done(((f32[128,2048]{1,0:T(8,128)}), f32[128,2048]{1,0:T(8,128)}) %all-reduce.10.cloned.1.call-update) | async-done | bytes 1048592 | tf_op jit(solution)/shard_map/psum | solution.py:161
  694.4 1.7 multiply_reduce_fusion
  696.1 1.7 multiply_add_fusion
  697.8 1.5 convolution_convert_fusion.2
  699.3 1.1 copy.55
  700.5 1.6 fusion.11
  702.1 1.7 multiply_reduce_fusion.1
  706.4 2.4 fusion.1
  709.1 17.1 convolution_bitcast_fusion
  726.3 2.5 fusion.32
  728.8 2.5 fusion.30
  731.4 5.5 fusion.22
  737.5 4.7 fusion.34
  742.3 14.3 fusion.49
  757.0 21.0 fusion.48
  779.9 1.6 fusion.16
  781.5 63.1 %all-reduce.2 = (f32[2048]{0:T(1024)S(1)}, f32[2048]{0:T(1024)S(1)}) all-reduce(f32[2048]{0:T(1024)S(1)} %get-tuple-element.46, f32[2048]{0:T(1024)S(1)} %get-tuple-element.44), channel_id=9, replica_groups=mesh['dp'=16,'tensor'=2] {'dp'}, use_global_device_ids=true, to_apply=%region_19.20.clone | all-reduce | flops 4096 | bytes 32768
  845.8 2.8 fusion.13
  848.6 235.4 %reduce-scatter.20.cloned.1.call-done = f32[128,4096]{0,1:T(8,128)} async-done(((f32[2048,4096]{0,1:T(8,128)}), f32[128,4096]{0,1:T(8,128)}) %reduce-scatter.20.cloned.1.call-update) | async-done | bytes 2097168 | tf_op jit(solution)/shard_map/reduce_scatter | solution.py:245
  1083.9 2.9 copy.59
  1086.8 62.2 %reduce-scatter.10.cloned.1.call-done = f32[128,256]{1,0:T(8,128)} async-done(((f32[2048,256]{1,0:T(8,128)}), f32[128,256]{1,0:T(8,128)}) %reduce-scatter.10.cloned.1.call-update) | async-done | bytes 131088 | tf_op jit(solution)/shard_map/reduce_scatter | solution.py:240
  1149.0 65.0 %reduce-scatter.12.cloned.1.call-done = f32[128,256]{1,0:T(8,128)} async-done(((f32[2048,256]{1,0:T(8,128)}), f32[128,256]{1,0:T(8,128)}) %reduce-scatter.12.cloned.1.call-update) | async-done | bytes 131088 | tf_op jit(solution)/shard_map/reduce_scatter | solution.py:241
  1214.1 106.9 %reduce-scatter.14.cloned.1.call-done = f32[128,1024]{1,0:T(8,128)} async-done(((f32[2048,1024]{1,0:T(8,128)}), f32[128,1024]{1,0:T(8,128)}) %reduce-scatter.14.cloned.1.call-update) | async-done | bytes 524304 | tf_op jit(solution)/shard_map/reduce_scatter | solution.py:242
  1321.0 107.6 %reduce-scatter.8.cloned.1.call-done = f32[128,1024]{1,0:T(8,128)} async-done(((f32[2048,1024]{1,0:T(8,128)}), f32[128,1024]{1,0:T(8,128)}) %reduce-scatter.8.cloned.1.call-update) | async-done | bytes 524304 | tf_op jit(solution)/shard_map/reduce_scatter | solution.py:239
  1428.6 334.9 %reduce-scatter.18.cloned.1.call-done = f32[128,4096]{1,0:T(8,128)} async-done(((f32[2048,4096]{1,0:T(8,128)}), f32[128,4096]{1,0:T(8,128)}) %reduce-scatter.18.cloned.1.call-update) | async-done | bytes 2097168 | tf_op jit(solution)/shard_map/reduce_scatter | solution.py:244
  1763.5 334.3 %reduce-scatter.16.cloned.1.call-done = f32[128,4096]{1,0:T(8,128)} async-done(((f32[2048,4096]{1,0:T(8,128)}), f32[128,4096]{1,0:T(8,128)}) %reduce-scatter.16.cloned.1.call-update) | async-done | bytes 2097168 | tf_op jit(solution)/shard_map/reduce_scatter | solution.py:243
  (109 shorter events, 14.9 us)
Async XLA Ops:
  7.2 134.1 %copy-start = (bf16[128,2048]{1,0:T(8,128)(2,1)S(1)}, bf16[128,2048]{1,0:T(8,128)(2,1)}, u32[]{:S(2)}) copy-start(bf16[128,2048]{1,0:T(8,128)(2,1)} %param.13) | copy-start | bytes 1572868
  7.2 43.6 %all-gather.10.cloned.1.call-start = ((), (), s32[]{:S(2)}) async-start(), calls=%async_computation.7 | async-start | bytes 1114112 | tf_op jit(solution)/shard_map/all_gather | solution.py:85
  7.9 81.8 %all-gather.12.cloned.1.call-start = ((), (), s32[]{:S(2)}) async-start(), calls=%async_computation.8 | async-start | bytes 1114112 | tf_op jit(solution)/shard_map/all_gather | solution.py:84
  8.7 132.6 %all-gather.14.cloned.1.call-start = ((), (), s32[]{:S(2)}) async-start(), calls=%async_computation.9 | async-start | bytes 4456448 | tf_op jit(solution)/shard_map/all_gather | solution.py:83
  9.4 182.9 %all-gather.16.cloned.1.call-start = ((), (), s32[]{:S(2)}) async-start(), calls=%async_computation.10 | async-start | bytes 4456448 | tf_op jit(solution)/shard_map/all_gather | solution.py:86
  10.0 225.8 %all-reduce.8.cloned.1.call-start = ((), (), s32[]{:S(2)}) async-start(), calls=%async_computation.11 | async-start | bytes 2097152 | tf_op jit(solution)/shard_map/psum | solution.py:129
  35.2 110.1 %copy-start.18 = (f32[128]{0:T(128)}, f32[128]{0:T(128)S(1)}, u32[]{:S(2)}) copy-start(f32[128]{0:T(128)S(1)} %add_rsqrt_fusion.1) | copy-start | bytes 1540
  52.6 94.0 %copy-start.13 = (bf16[128,256]{0,1:T(8,128)(2,1)}, bf16[128,256]{0,1:T(8,128)(2,1)S(1)}, u32[]{:S(2)}) copy-start(bf16[128,256]{0,1:T(8,128)(2,1)S(1)} %copy.51) | copy-start | bytes 196612
  91.8 54.9 %copy-start.14 = (bf16[128,4,32]{0,2,1:T(8,128)(2,1)}, bf16[128,4,32]{0,2,1:T(8,128)(2,1)S(1)}, u32[]{:S(2)}) copy-start(bf16[128,4,32]{0,2,1:T(8,128)(2,1)S(1)} %get-tuple-element.63) | copy-start | bytes 98308
  91.8 54.8 %copy-start.16 = (bf16[128,4,32]{0,2,1:T(8,128)(2,1)}, bf16[128,4,32]{0,2,1:T(8,128)(2,1)S(1)}, u32[]{:S(2)}) copy-start(bf16[128,4,32]{0,2,1:T(8,128)(2,1)S(1)} %get-tuple-element.64) | copy-start | bytes 98308
  145.4 0.7 copy-start.9
  145.4 1.0 copy-start.11
  146.4 50.6 %copy-start.2 = (f32[4,4,128,128]{2,3,1,0:T(8,128)}, f32[4,4,128,128]{2,3,1,0:T(8,128)S(1)}, u32[]{:S(2)}) copy-start(f32[4,4,128,128]{2,3,1,0:T(8,128)S(1)} %get-tuple-element.69) | copy-start | bytes 3145732
  147.0 51.4 %copy-start.6 = (bf16[4,64,4,128]{3,1,2,0:T(8,128)(2,1)}, bf16[4,64,4,128]{3,1,2,0:T(8,128)(2,1)S(1)}, u32[]{:S(2)}) copy-start(bf16[4,64,4,128]{3,1,2,0:T(8,128)(2,1)S(1)} %convolution_convert_fusion.1) | copy-start | bytes 786436
  192.3 6.9 copy-start.20
  197.0 167.3 %all-gather.20.cloned.1.call-start = ((), (), s32[]{:S(2)}) async-start(), calls=%async_computation.13 | async-start | bytes 17825792 | tf_op jit(solution)/shard_map/all_gather | solution.py:133
  197.6 293.5 %all-gather.18.cloned.1.call-start = ((), (), s32[]{:S(2)}) async-start(), calls=%async_computation.12 | async-start | bytes 17825792 | tf_op jit(solution)/shard_map/all_gather | solution.py:132
  198.3 419.5 %all-gather.22.cloned.1.call-start = ((), (), s32[]{:S(2)}) async-start(), calls=%async_computation.14 | async-start | bytes 17825792 | tf_op jit(solution)/shard_map/all_gather | solution.py:134
  199.1 495.3 %all-reduce.10.cloned.1.call-start = ((), (), s32[]{:S(2)}) async-start(), calls=%async_computation.15 | async-start | bytes 2097152 | tf_op jit(solution)/shard_map/psum | solution.py:161
  629.8 26.3 %copy-start.5 = (bf16[128,4096]{1,0:T(8,128)(2,1)}, bf16[128,4096]{1,0:T(8,128)(2,1)S(1)}, u32[]{:S(2)}) copy-start(bf16[128,4096]{1,0:T(8,128)(2,1)S(1)} %get-tuple-element.56) | copy-start | bytes 3145732
  655.9 123.9 %all-reduce.12.cloned.1.call-start = ((), (), s32[]{:S(2)}) async-start(), calls=%async_computation.23 | async-start | bytes 2097152 | tf_op jit(solution)/shard_map/psum | solution.py:144
  694.4 3.4 copy-start.4
  700.4 3.4 copy-start.3
  700.4 3.7 copy-start.10
  700.4 3.7 copy-start.12
  700.5 4.0 copy-start.15
  700.5 4.0 copy-start.17
  702.1 2.7 copy-start.7
  703.9 1.5 copy-start.8
  704.1 2.3 copy-start.1
  708.8 375.1 %reduce-scatter.20.cloned.1.call-start = ((), (), s32[]{:S(2)}) async-start(), calls=%async_computation.22 | async-start | bytes 35651584 | tf_op jit(solution)/shard_map/reduce_scatter | solution.py:245
  726.2 422.8 %reduce-scatter.10.cloned.1.call-start = ((), (), s32[]{:S(2)}) async-start(), calls=%async_computation.17 | async-start | bytes 2228224 | tf_op jit(solution)/shard_map/reduce_scatter | solution.py:240
  728.8 485.3 %reduce-scatter.12.cloned.1.call-start = ((), (), s32[]{:S(2)}) async-start(), calls=%async_computation.18 | async-start | bytes 2228224 | tf_op jit(solution)/shard_map/reduce_scatter | solution.py:241
  731.4 589.6 %reduce-scatter.14.cloned.1.call-start = ((), (), s32[]{:S(2)}) async-start(), calls=%async_computation.19 | async-start | bytes 8912896 | tf_op jit(solution)/shard_map/reduce_scatter | solution.py:242
  736.9 0.7 copy-start.19
  736.9 691.7 %reduce-scatter.8.cloned.1.call-start = ((), (), s32[]{:S(2)}) async-start(), calls=%async_computation.16 | async-start | bytes 8912896 | tf_op jit(solution)/shard_map/reduce_scatter | solution.py:239
  742.2 1021.3 %reduce-scatter.18.cloned.1.call-start = ((), (), s32[]{:S(2)}) async-start(), calls=%async_computation.21 | async-start | bytes 35651584 | tf_op jit(solution)/shard_map/reduce_scatter | solution.py:244
  756.7 1341.2 %reduce-scatter.16.cloned.1.call-start = ((), (), s32[]{:S(2)}) async-start(), calls=%async_computation.20 | async-start | bytes 35651584 | tf_op jit(solution)/shard_map/reduce_scatter | solution.py:243
  777.9 0.7 copy-start.21
Sparse Core Ops, SparseCore 0:
  10.2 40.5 all-gather.9
  52.9 36.7 all-gather.11
  91.9 49.3 all-gather.13
  143.3 48.8 all-gather.15
  197.1 38.6 all-reduce.7
  237.8 126.4 all-gather.19
  366.4 124.5 all-gather.17
  493.2 124.5 all-gather.21
  656.1 38.2 all-reduce.9
  708.9 40.0 all-reduce.11
  753.3 330.5 reduce-scatter.19
  1088.1 60.8 reduce-scatter.9
  1153.3 60.6 reduce-scatter.11
  1218.6 102.3 reduce-scatter.13
  1325.5 103.0 reduce-scatter.7
  1433.3 330.1 reduce-scatter.17
  1768.2 329.6 reduce-scatter.15
where the time goes:
time: 2110 us; the launch traced here: 2100 us
  waiting for transfers between devices  1800 us (85%)
  matrix products  159 us (8%)
  blocking collectives  106 us (5%)
    reduce_scatter x1, waiting for transfers between devices, on_device(): lax.psum_scatter(up_grad, 'dp', scatter_dimension=0, tiled=True)  335 us
    reduce_scatter x1, waiting for transfers between devices, on_device(): lax.psum_scatter(gate_grad, 'dp', scatter_dimension=0, tiled=True)  334 us
    reduce_scatter x1, waiting for transfers between devices, on_device(): lax.psum_scatter(down_grad, 'dp', scatter_dimension=0, tiled=True)  235 us
    all_gather x1, waiting for transfers between devices, on_device(): lax.all_gather(w_up, 'dp', axis=0, tiled=True)  127 us
    all_gather x1, waiting for transfers between devices, on_device(): lax.all_gather(w_down, 'dp', axis=0, tiled=True)  117 us
    all_gather x1, waiting for transfers between devices, on_device(): lax.all_gather(w_gate, 'dp', axis=0, tiled=True)  117 us
    reduce_scatter x1, waiting for transfers between devices, on_device(): lax.psum_scatter(query_grad, 'dp', scatter_dimension=0, tiled=True)  108 us
    reduce_scatter x1, waiting for transfers between devices, on_device(): lax.psum_scatter(out_proj_grad, 'dp', scatter_dimension=0, tiled=True)  107 us
  transfers between devices with their start and end apart: 17, of which 16 were waited for; matrix products, arithmetic and copies ran while one was open for 6% of the time, Pallas kernels for 0%

commit v1 on v0

--- a/solution.py
+++ b/solution.py
@@ -10,6 +10,16 @@
 norm_eps = 1e-05
 rope_base = 500000.0
 masked_score = -1e30
+
+
+def carry_stages_all(body, array_dim):
+    body = jnp.moveaxis(body, 0, array_dim)
+    item_now = body.shape
+    return body.reshape(
+        *item_now[:array_dim],
+        item_now[array_dim] * item_now[array_dim + 1],
+        *item_now[array_dim + 2 :]
+    )
 
 
 def rope_freqs(head_dim):
@@ -128,10 +138,26 @@
     )
     attn_out = lax.psum(dot_last(attended, out_full), "tensor")
     middle = residual + attn_out
+
+    def find_corner_up(x0, axis_id, d0):
+        shares = jax.lax.psum(1, axis_id)
+        pool = tuple(((q, (q + 1) % shares) for q in range(shares)))
+        cards = tuple(((dd, c) for c, dd in pool))
+        odd, known = ([], [])
+        for pp in range(shares - 1):
+            if pp % 2 == 0:
+                odd.append(jax.lax.ppermute(odd[-1] if odd else x0, axis_id, pool))
+            else:
+                known.append(jax.lax.ppermute(known[-1] if known else x0, axis_id, cards))
+        val = jnp.stack([*odd[::-1], x0, *known])
+        piece_now = jax.lax.axis_index(axis_id) - len(odd)
+        val = val[(jnp.arange(shares) - piece_now) % shares]
+        return carry_stages_all(val, d0)
+
     gate_full, up_full, down_full, gain_two = (
         lax.all_gather(w_gate, "dp", axis=0, tiled=True),
         lax.all_gather(w_up, "dp", axis=0, tiled=True),
-        lax.all_gather(w_down, "dp", axis=0, tiled=True),
+        find_corner_up(w_down, axis_id="dp", d0=0),
         lax.all_gather(mlp_gain, "dp", axis=0, tiled=True),
     )
     gain_two = gain_two.astype(jnp.float32)

time: 2110 us -> 2200 us (1.043)
  starting transfers between devices: 1.14 us -> 131 us
  waiting for transfers between devices: 1800 us -> 1690 us
  local copies, waits for them, and re-layouts: 8.4 us -> 53.5 us
    ppermute x0 -> x15, starting transfers between devices: none -> 130 us  [the longest x8 122 us: find_corner_up(): odd.append(jax.lax.ppermute(odd[-1] if odd else x0, axis_id, pool))]
    all_gather x1, waiting for transfers between devices: 117 us -> 0.02 us  [on_device(): lax.all_gather(w_gate, 'dp', axis=0, tiled=True)]
    ppermute x0 -> x15, waiting for transfers between devices: none -> 77.7 us  [the longest x8 77.7 us: find_corner_up(): odd.append(jax.lax.ppermute(odd[-1] if odd else x0, axis_id, pool))]
    all_gather x1, waiting for transfers between devices: 127 us -> 87.2 us  [on_device(): lax.all_gather(w_up, 'dp', axis=0, tiled=True)]
    unnamed x48 -> x73, local copies, waits for them, and re-layouts: 7.18 us -> 36.6 us
  transfers between devices with their start and end apart: 17 -> 32, of which waited for: 16 -> 21; matrix products, arithmetic and copies ran while one was open for 6% -> 9% of each run, Pallas kernels for 0% -> 0%
where the time goes in v1:
time: 2200 us; the launch traced here: 2190 us
  waiting for transfers between devices  1690 us (77%)
  matrix products  168 us (8%)
  starting transfers between devices  131 us (6%)
  blocking collectives  120 us (5%)
  local copies, waits for them, and re-layouts  53.5 us (2%)
    reduce_scatter x1, waiting for transfers between devices, on_device(): lax.psum_scatter(gate_grad, 'dp', scatter_dimension=0, tiled=True)  335 us
    reduce_scatter x1, waiting for transfers between devices, on_device(): lax.psum_scatter(up_grad, 'dp', scatter_dimension=0, tiled=True)  334 us
    reduce_scatter x1, waiting for transfers between devices, on_device(): lax.psum_scatter(down_grad, 'dp', scatter_dimension=0, tiled=True)  235 us
    ppermute x8, starting transfers between devices, find_corner_up(): odd.append(jax.lax.ppermute(odd[-1] if odd else x0, axis_id, pool))  122 us
    all_gather x1, waiting for transfers between devices, on_device(): lax.all_gather(w_down, 'dp', axis=0, tiled=True)  117 us
    reduce_scatter x1, waiting for transfers between devices, on_device(): lax.psum_scatter(out_proj_grad, 'dp', scatter_dimension=0, tiled=True)  108 us
    reduce_scatter x1, waiting for transfers between devices, on_device(): lax.psum_scatter(query_grad, 'dp', scatter_dimension=0, tiled=True)  107 us
    all_gather x1, waiting for transfers between devices, on_device(): lax.all_gather(w_up, 'dp', axis=0, tiled=True)  87.2 us
  transfers between devices with their start and end apart: 32, of which 21 were waited for; matrix products, arithmetic and copies ran while one was open for 9% of the time, Pallas kernels for 0%

profile of v1, /device:TPU:0, one launch (start us, length us, event | category | flops | bytes accessed | tf_op | source)
XLA Modules:
  0.0 2191.5 jit_solution(11989202208589480372)
XLA Ops:
  10.0 23.3 %all-gather = bf16[16,1,128]{2,1,0:T(2,128)(2,1)S(1)} all-gather(bf16[1,1,128]{2,1,0:T(2,128)(2,1)} %bitcast.170), channel_id=1, replica_groups=mesh['dp'=16,'tensor'=2] {'dp'}, dimensions={0}, use_global_device_ids=true | all-gather | bytes 4352 | tf_op jit(solution)/shard_map/all_gather | solution.py:97
  36.2 14.5 all-gather.10.cloned.1.call-done
  52.6 37.1 %all-gather.12.cloned.1.call-done = bf16[2048,256]{1,0:T(8,128)(2,1)} async-done(((bf16[128,256]{1,0:T(8,128)(2,1)}), bf16[2048,256]{1,0:T(8,128)(2,1)}) %all-gather.12.cloned.1.call-update) | async-done | bytes 1048592 | tf_op jit(solution)/shard_map/all_gather | solution.py:94
  91.8 49.5 %all-gather.14.cloned.1.call-done = bf16[2048,1024]{1,0:T(8,128)(2,1)} async-done(((bf16[128,1024]{1,0:T(8,128)(2,1)}), bf16[2048,1024]{1,0:T(8,128)(2,1)}) %all-gather.14.cloned.1.call-update) | async-done | bytes 4194320 | tf_op jit(solution)/shard_map/all_gather | solution.py:93
  141.3 4.1 fusion.38
  147.3 45.0 %all-gather.16.cloned.1.call-done = bf16[2048,1024]{1,0:T(8,128)(2,1)} async-done(((bf16[128,1024]{1,0:T(8,128)(2,1)}), bf16[2048,1024]{1,0:T(8,128)(2,1)}) %all-gather.16.cloned.1.call-update) | async-done | bytes 4194320 | tf_op jit(solution)/shard_map/all_gather | solution.py:96
  192.3 4.7 fusion.44
  199.5 16.7 collective-permute-done
  216.2 4.4 collective-permute-start.8
  220.6 12.6 collective-permute-done.1
  233.2 3.9 collective-permute-start.2
  238.6 11.6 collective-permute-done.2
  250.2 23.6 %collective-permute-start.3 = (bf16[128,4096]{1,0:T(8,128)(2,1)S(1)}, bf16[128,4096]{1,0:T(8,128)(2,1)S(1)}, u32[]{:S(2)}, u32[]{:S(2)}) collective-permute-start(bf16[128,4096]{1,0:T(8,128)(2,1)S(1)} %collective-permute-done.2), channel_id=1, source_target_pairs={{0,2},{2,4},{4,6},{6,8},{8,10},{10,12},{12,14},{14,16},{16,18},{18... | collective-permute-start | bytes 3145736 | tf_op jit(solution)/shard_map/ppermute | solution.py:149
  274.8 14.9 collective-permute-done.3
  289.7 9.3 collective-permute-start.4
  300.8 12.5 collective-permute-done.4
  313.3 31.5 %collective-permute-start.5 = (bf16[128,4096]{1,0:T(8,128)(2,1)S(1)}, bf16[128,4096]{1,0:T(8,128)(2,1)S(1)}, u32[]{:S(2)}, u32[]{:S(2)}) collective-permute-start(bf16[128,4096]{1,0:T(8,128)(2,1)S(1)} %collective-permute-done.4), channel_id=1, source_target_pairs={{0,2},{2,4},{4,6},{6,8},{8,10},{10,12},{12,14},{14,16},{16,18},{18... | collective-permute-start | bytes 3145736 | tf_op jit(solution)/shard_map/ppermute | solution.py:149
  345.8 7.0 collective-permute-done.5
  352.8 37.9 %collective-permute-start.6 = (bf16[128,4096]{1,0:T(8,128)(2,1)S(1)}, bf16[128,4096]{1,0:T(8,128)(2,1)}, u32[]{:S(2)}, u32[]{:S(2)}) collective-permute-start(bf16[128,4096]{1,0:T(8,128)(2,1)S(1)} %collective-permute-done.5), channel_id=1, source_target_pairs={{0,2},{2,4},{4,6},{6,8},{8,10},{10,12},{12,14},{14,16},{16,18},{18... | collective-permute-start | bytes 3145736 | tf_op jit(solution)/shard_map/ppermute | solution.py:149
  393.2 15.8 collective-permute-start.7
  409.0 32.9 %all-gather.1 = bf16[16,1,128]{2,1,0:T(2,128)(2,1)S(1)} all-gather(bf16[1,1,128]{2,1,0:T(2,128)(2,1)S(1)} %bitcast.171), channel_id=1, replica_groups=mesh['dp'=16,'tensor'=2] {'dp'}, dimensions={0}, use_global_device_ids=true | all-gather | bytes 4352 | tf_op jit(solution)/shard_map/all_gather | solution.py:161
  472.0 9.5 fusion.45
  481.4 87.2 %all-gather.20.cloned.1.call-done = bf16[2048,4096]{1,0:T(8,128)(2,1)} async-done(((bf16[128,4096]{1,0:T(8,128)(2,1)}), bf16[2048,4096]{1,0:T(8,128)(2,1)}) %all-gather.20.cloned.1.call-update) | async-done | bytes 16777232 | tf_op jit(solution)/shard_map/all_gather | solution.py:159
  568.7 9.4 fusion.46
  578.1 117.4 %all-gather.22.cloned.1.call-done = bf16[2048,4096]{1,0:T(8,128)(2,1)} async-done(((bf16[128,4096]{1,0:T(8,128)(2,1)}), bf16[2048,4096]{1,0:T(8,128)(2,1)}) %all-gather.22.cloned.1.call-update) | async-done | bytes 16777232 | tf_op jit(solution)/shard_map/all_gather | solution.py:177
  695.5 11.9 multiply_convert_fusion
  707.4 13.2 fusion.47
  720.6 12.9 convolution_add_fusion.1
  735.9 13.4 gather_fusion
  749.3 12.2 convolution_convert_fusion
  761.6 10.4 all-reduce.10.cloned.1.call-done
  775.3 3.6 convolution_convert_fusion.2
  790.5 4.5 fusion.1
  795.3 17.1 convolution_bitcast_fusion
  817.7 5.3 fusion.36
  823.1 5.5 fusion.22
  828.7 14.4 fusion.50
  843.4 21.0 fusion.51
  867.9 63.7 %all-reduce.2 = (f32[2048]{0:T(1024)S(1)}, f32[2048]{0:T(1024)S(1)}) all-reduce(f32[2048]{0:T(1024)S(1)} %get-tuple-element.46, f32[2048]{0:T(1024)S(1)} %get-tuple-element.44), channel_id=9, replica_groups=mesh['dp'=16,'tensor'=2] {'dp'}, use_global_device_ids=true, to_apply=%region_19.20.clone | all-reduce | flops 4096 | bytes 32768
  932.7 2.8 fusion.13
  935.5 235.4 %reduce-scatter.20.cloned.1.call-done = f32[128,4096]{0,1:T(8,128)} async-done(((f32[2048,4096]{0,1:T(8,128)}), f32[128,4096]{0,1:T(8,128)}) %reduce-scatter.20.cloned.1.call-update) | async-done | bytes 2097168 | tf_op jit(solution)/shard_map/reduce_scatter | solution.py:271
  1170.9 2.9 copy.59
  1173.7 62.1 %reduce-scatter.10.cloned.1.call-done = f32[128,256]{1,0:T(8,128)} async-done(((f32[2048,256]{1,0:T(8,128)}), f32[128,256]{1,0:T(8,128)}) %reduce-scatter.10.cloned.1.call-update) | async-done | bytes 131088 | tf_op jit(solution)/shard_map/reduce_scatter | solution.py:266
  1235.9 65.0 %reduce-scatter.12.cloned.1.call-done = f32[128,256]{1,0:T(8,128)} async-done(((f32[2048,256]{1,0:T(8,128)}), f32[128,256]{1,0:T(8,128)}) %reduce-scatter.12.cloned.1.call-update) | async-done | bytes 131088 | tf_op jit(solution)/shard_map/reduce_scatter | solution.py:267
  1300.9 107.0 %reduce-scatter.8.cloned.1.call-done = f32[128,1024]{1,0:T(8,128)} async-done(((f32[2048,1024]{1,0:T(8,128)}), f32[128,1024]{1,0:T(8,128)}) %reduce-scatter.8.cloned.1.call-update) | async-done | bytes 524304 | tf_op jit(solution)/shard_map/reduce_scatter | solution.py:265
  1407.9 107.6 %reduce-scatter.14.cloned.1.call-done = f32[128,1024]{1,0:T(8,128)} async-done(((f32[2048,1024]{1,0:T(8,128)}), f32[128,1024]{1,0:T(8,128)}) %reduce-scatter.14.cloned.1.call-update) | async-done | bytes 524304 | tf_op jit(solution)/shard_map/reduce_scatter | solution.py:268
  1515.5 334.9 %reduce-scatter.16.cloned.1.call-done = f32[128,4096]{1,0:T(8,128)} async-done(((f32[2048,4096]{1,0:T(8,128)}), f32[128,4096]{1,0:T(8,128)}) %reduce-scatter.16.cloned.1.call-update) | async-done | bytes 2097168 | tf_op jit(solution)/shard_map/reduce_scatter | solution.py:269
  1850.4 334.3 %reduce-scatter.18.cloned.1.call-done = f32[128,4096]{1,0:T(8,128)} async-done(((f32[2048,4096]{1,0:T(8,128)}), f32[128,4096]{1,0:T(8,128)}) %reduce-scatter.18.cloned.1.call-update) | async-done | bytes 2097168 | tf_op jit(solution)/shard_map/reduce_scatter | solution.py:270
  (168 shorter events, 78.2 us)
Async XLA Ops:
  7.2 192.0 %copy-start.3 = (bf16[128,4096]{1,0:T(8,128)(2,1)S(1)}, bf16[128,4096]{1,0:T(8,128)(2,1)}, u32[]{:S(2)}) copy-start(bf16[128,4096]{1,0:T(8,128)(2,1)} %param.22) | copy-start | bytes 3145732
  7.2 401.9 %copy-start.25 = (bf16[128]{0:T(256)(128)(2,1)S(1)}, bf16[128]{0:T(256)(128)(2,1)}, u32[]{:S(2)}) copy-start(bf16[128]{0:T(256)(128)(2,1)} %param.24) | copy-start | bytes 772
  7.2 43.6 %all-gather.10.cloned.1.call-start = ((), (), s32[]{:S(2)}) async-start(), calls=%async_computation.7 | async-start | bytes 1114112 | tf_op jit(solution)/shard_map/all_gather | solution.py:95
  7.9 81.8 %all-gather.12.cloned.1.call-start = ((), (), s32[]{:S(2)}) async-start(), calls=%async_computation.8 | async-start | bytes 1114112 | tf_op jit(solution)/shard_map/all_gather | solution.py:94
  8.7 132.7 %all-gather.14.cloned.1.call-start = ((), (), s32[]{:S(2)}) async-start(), calls=%async_computation.9 | async-start | bytes 4456448 | tf_op jit(solution)/shard_map/all_gather | solution.py:93
  9.4 182.9 %all-gather.16.cloned.1.call-start = ((), (), s32[]{:S(2)}) async-start(), calls=%async_computation.10 | async-start | bytes 4456448 | tf_op jit(solution)/shard_map/all_gather | solution.py:96
  10.0 460.3 %all-reduce.8.cloned.1.call-start = ((), (), s32[]{:S(2)}) async-start(), calls=%async_computation.11 | async-start | bytes 2097152 | tf_op jit(solution)/shard_map/psum | solution.py:139
  35.3 110.2 %copy-start.23 = (f32[128]{0:T(128)}, f32[128]{0:T(128)S(1)}, u32[]{:S(2)}) copy-start(f32[128]{0:T(128)S(1)} %add_rsqrt_fusion.1) | copy-start | bytes 1540
  52.6 146.5 %copy-start.20 = (bf16[128,256]{0,1:T(8,128)(2,1)}, bf16[128,256]{0,1:T(8,128)(2,1)S(1)}, u32[]{:S(2)}) copy-start(bf16[128,256]{0,1:T(8,128)(2,1)S(1)} %copy.51) | copy-start | bytes 196612
  91.8 107.3 %copy-start.21 = (bf16[128,4,32]{0,2,1:T(8,128)(2,1)}, bf16[128,4,32]{0,2,1:T(8,128)(2,1)S(1)}, u32[]{:S(2)}) copy-start(bf16[128,4,32]{0,2,1:T(8,128)(2,1)S(1)} %get-tuple-element.63) | copy-start | bytes 98308
  91.8 107.3 %copy-start.22 = (bf16[128,4,32]{0,2,1:T(8,128)(2,1)}, bf16[128,4,32]{0,2,1:T(8,128)(2,1)S(1)}, u32[]{:S(2)}) copy-start(bf16[128,4,32]{0,2,1:T(8,128)(2,1)S(1)} %get-tuple-element.64) | copy-start | bytes 98308
  145.6 315.8 %copy-start.18 = (bf16[128,16,32]{0,2,1:T(8,128)(2,1)}, bf16[128,16,32]{0,2,1:T(8,128)(2,1)S(1)}, u32[]{:S(2)}) copy-start(bf16[128,16,32]{0,2,1:T(8,128)(2,1)S(1)} %get-tuple-element.59) | copy-start | bytes 393220
  145.6 315.8 %copy-start.19 = (bf16[128,16,32]{0,2,1:T(8,128)(2,1)}, bf16[128,16,32]{0,2,1:T(8,128)(2,1)S(1)}, u32[]{:S(2)}) copy-start(bf16[128,16,32]{0,2,1:T(8,128)(2,1)S(1)} %get-tuple-element.60) | copy-start | bytes 393220
  147.3 49.8 %copy-start.4 = (bf16[4,64,4,128]{3,1,2,0:T(8,128)(2,1)}, bf16[4,64,4,128]{3,1,2,0:T(8,128)(2,1)S(1)}, u32[]{:S(2)}) copy-start(bf16[4,64,4,128]{3,1,2,0:T(8,128)(2,1)S(1)} %convolution_convert_fusion.1) | copy-start | bytes 786436
  197.0 275.0 %all-gather.18.cloned.1.call-start = ((), (), s32[]{:S(2)}) async-start(), calls=%async_computation.12 | async-start | bytes 17825792 | tf_op jit(solution)/shard_map/all_gather | solution.py:158
  197.6 272.7 %copy-start = (bf16[128,2048]{1,0:T(8,128)(2,1)S(1)}, bf16[128,2048]{1,0:T(8,128)(2,1)}, u32[]{:S(2)}) copy-start(bf16[128,2048]{1,0:T(8,128)(2,1)} %param.13) | copy-start | bytes 1572868
  197.6 371.1 %all-gather.20.cloned.1.call-start = ((), (), s32[]{:S(2)}) async-start(), calls=%async_computation.13 | async-start | bytes 17825792 | tf_op jit(solution)/shard_map/all_gather | solution.py:159
  198.3 497.1 %all-gather.22.cloned.1.call-start = ((), (), s32[]{:S(2)}) async-start(), calls=%async_computation.14 | async-start | bytes 17825792 | tf_op jit(solution)/shard_map/all_gather | solution.py:177
  199.1 572.9 %all-reduce.10.cloned.1.call-start = ((), (), s32[]{:S(2)}) async-start(), calls=%async_computation.15 | async-start | bytes 2097152 | tf_op jit(solution)/shard_map/psum | solution.py:187
  199.2 17.0 collective-permute-start
  216.1 17.0 collective-permute-start.1
  216.2 21.0 collective-permute-start.8
  233.2 40.6 %copy-start.7 = (bf16[128,4096]{1,0:T(8,128)(2,1)}, bf16[128,4096]{1,0:T(8,128)(2,1)S(1)}, u32[]{:S(2)}) copy-start(bf16[128,4096]{1,0:T(8,128)(2,1)S(1)} %collective-permute-done.1) | copy-start | bytes 3145732
  233.2 17.0 collective-permute-start.2
  238.1 35.7 %collective-permute-start.9 = (bf16[128,4096]{1,0:T(8,128)(2,1)S(1)}, bf16[128,4096]{1,0:T(8,128)(2,1)S(1)}, u32[]{:S(2)}, u32[]{:S(2)}) collective-permute-start(bf16[128,4096]{1,0:T(8,128)(2,1)S(1)} %collective-permute-done.8), channel_id=1, source_target_pairs={{2,0},{4,2},{6,4},{8,6},{10,8},{12,10},{14,12},{16,14},{18,16},{20... | collective-permute-start | bytes 3145736 | tf_op jit(solution)/shard_map/ppermute | solution.py:151
  250.2 48.9 %copy-start.10 = (bf16[128,4096]{1,0:T(8,128)(2,1)}, bf16[128,4096]{1,0:T(8,128)(2,1)S(1)}, u32[]{:S(2)}) copy-start(bf16[128,4096]{1,0:T(8,128)(2,1)S(1)} %collective-permute-done.2) | copy-start | bytes 3145732
  250.2 39.5 %collective-permute-start.3 = (bf16[128,4096]{1,0:T(8,128)(2,1)S(1)}, bf16[128,4096]{1,0:T(8,128)(2,1)S(1)}, u32[]{:S(2)}, u32[]{:S(2)}) collective-permute-start(bf16[128,4096]{1,0:T(8,128)(2,1)S(1)} %collective-permute-done.2), channel_id=1, source_target_pairs={{0,2},{2,4},{4,6},{6,8},{8,10},{10,12},{12,14},{14,16},{16,18},{18... | collective-permute-start | bytes 3145736 | tf_op jit(solution)/shard_map/ppermute | solution.py:149
  273.8 25.2 %collective-permute-start.10 = (bf16[128,4096]{1,0:T(8,128)(2,1)S(1)}, bf16[128,4096]{1,0:T(8,128)(2,1)S(1)}, u32[]{:S(2)}, u32[]{:S(2)}) collective-permute-start(bf16[128,4096]{1,0:T(8,128)(2,1)S(1)} %collective-permute-done.9), channel_id=1, source_target_pairs={{2,0},{4,2},{6,4},{8,6},{10,8},{12,10},{14,12},{16,14},{18,16},{20... | collective-permute-start | bytes 3145736 | tf_op jit(solution)/shard_map/ppermute | solution.py:151
  289.7 101.1 %copy-start.15 = (bf16[128,4096]{1,0:T(8,128)(2,1)}, bf16[128,4096]{1,0:T(8,128)(2,1)S(1)}, u32[]{:S(2)}) copy-start(bf16[128,4096]{1,0:T(8,128)(2,1)S(1)} %collective-permute-done.3) | copy-start | bytes 3145732
  289.7 23.6 %collective-permute-start.4 = (bf16[128,4096]{1,0:T(8,128)(2,1)S(1)}, bf16[128,4096]{1,0:T(8,128)(2,1)S(1)}, u32[]{:S(2)}, u32[]{:S(2)}) collective-permute-start(bf16[128,4096]{1,0:T(8,128)(2,1)S(1)} %collective-permute-done.3), channel_id=1, source_target_pairs={{0,2},{2,4},{4,6},{6,8},{8,10},{10,12},{12,14},{14,16},{16,18},{18... | collective-permute-start | bytes 3145736 | tf_op jit(solution)/shard_map/ppermute | solution.py:149
  299.1 45.7 %collective-permute-start.11 = (bf16[128,4096]{1,0:T(8,128)(2,1)S(1)}, bf16[128,4096]{1,0:T(8,128)(2,1)S(1)}, u32[]{:S(2)}, u32[]{:S(2)}) collective-permute-start(bf16[128,4096]{1,0:T(8,128)(2,1)S(1)} %collective-permute-done.10), channel_id=1, source_target_pairs={{2,0},{4,2},{6,4},{8,6},{10,8},{12,10},{14,12},{16,14},{18,16},{20... | collective-permute-start | bytes 3145736 | tf_op jit(solution)/shard_map/ppermute | solution.py:151
  313.3 77.5 %copy-start.16 = (bf16[128,4096]{1,0:T(8,128)(2,1)}, bf16[128,4096]{1,0:T(8,128)(2,1)S(1)}, u32[]{:S(2)}) copy-start(bf16[128,4096]{1,0:T(8,128)(2,1)S(1)} %collective-permute-done.4) | copy-start | bytes 3145732
  313.3 39.5 %collective-permute-start.5 = (bf16[128,4096]{1,0:T(8,128)(2,1)S(1)}, bf16[128,4096]{1,0:T(8,128)(2,1)S(1)}, u32[]{:S(2)}, u32[]{:S(2)}) collective-permute-start(bf16[128,4096]{1,0:T(8,128)(2,1)S(1)} %collective-permute-done.4), channel_id=1, source_target_pairs={{0,2},{2,4},{4,6},{6,8},{8,10},{10,12},{12,14},{14,16},{16,18},{18... | collective-permute-start | bytes 3145736 | tf_op jit(solution)/shard_map/ppermute | solution.py:149
  345.8 45.0 %collective-permute-start.12 = (bf16[128,4096]{1,0:T(8,128)(2,1)S(1)}, bf16[128,4096]{1,0:T(8,128)(2,1)}, u32[]{:S(2)}, u32[]{:S(2)}) collective-permute-start(bf16[128,4096]{1,0:T(8,128)(2,1)S(1)} %collective-permute-done.11), channel_id=1, source_target_pairs={{2,0},{4,2},{6,4},{8,6},{10,8},{12,10},{14,12},{16,14},{18,16},{20... | collective-permute-start | bytes 3145736 | tf_op jit(solution)/shard_map/ppermute | solution.py:151
  352.8 40.4 %copy-start.17 = (bf16[128,4096]{1,0:T(8,128)(2,1)}, bf16[128,4096]{1,0:T(8,128)(2,1)S(1)}, u32[]{:S(2)}) copy-start(bf16[128,4096]{1,0:T(8,128)(2,1)S(1)} %collective-permute-done.5) | copy-start | bytes 3145732
  352.8 40.4 %collective-permute-start.6 = (bf16[128,4096]{1,0:T(8,128)(2,1)S(1)}, bf16[128,4096]{1,0:T(8,128)(2,1)}, u32[]{:S(2)}, u32[]{:S(2)}) collective-permute-start(bf16[128,4096]{1,0:T(8,128)(2,1)S(1)} %collective-permute-done.5), channel_id=1, source_target_pairs={{0,2},{2,4},{4,6},{6,8},{8,10},{10,12},{12,14},{14,16},{16,18},{18... | collective-permute-start | bytes 3145736 | tf_op jit(solution)/shard_map/ppermute | solution.py:149
  390.8 51.3 %collective-permute-start.13 = (bf16[128,4096]{1,0:T(8,128)(2,1)}, bf16[128,4096]{1,0:T(8,128)(2,1)}, u32[]{:S(2)}, u32[]{:S(2)}) collective-permute-start(bf16[128,4096]{1,0:T(8,128)(2,1)} %collective-permute-done.12), channel_id=1, source_target_pairs={{2,0},{4,2},{6,4},{8,6},{10,8},{12,10},{14,12},{16,14},{18,16},{20... | collective-permute-start | bytes 3145736 | tf_op jit(solution)/shard_map/ppermute | solution.py:151
  393.2 49.6 %collective-permute-start.7 = (bf16[128,4096]{1,0:T(8,128)(2,1)}, bf16[128,4096]{1,0:T(8,128)(2,1)}, u32[]{:S(2)}, u32[]{:S(2)}) collective-permute-start(bf16[128,4096]{1,0:T(8,128)(2,1)} %collective-permute-done.6), channel_id=1, source_target_pairs={{0,2},{2,4},{4,6},{6,8},{8,10},{10,12},{12,14},{14,16},{16,18},{18... | collective-permute-start | bytes 3145736 | tf_op jit(solution)/shard_map/ppermute | solution.py:149
  442.1 291.5 %collective-permute-start.14 = (bf16[128,4096]{1,0:T(8,128)(2,1)}, bf16[128,4096]{1,0:T(8,128)(2,1)}, u32[]{:S(2)}, u32[]{:S(2)}) collective-permute-start(bf16[128,4096]{1,0:T(8,128)(2,1)} %collective-permute-done.13), channel_id=1, source_target_pairs={{2,0},{4,2},{6,4},{8,6},{10,8},{12,10},{14,12},{16,14},{18,16},{20... | collective-permute-start | bytes 3145736 | tf_op jit(solution)/shard_map/ppermute | solution.py:151
  707.4 42.0 %copy-start.2 = (bf16[128,4096]{1,0:T(8,128)(2,1)}, bf16[128,4096]{1,0:T(8,128)(2,1)S(1)}, u32[]{:S(2)}) copy-start(bf16[128,4096]{1,0:T(8,128)(2,1)S(1)} %get-tuple-element.56) | copy-start | bytes 3145732
  733.6 132.8 %all-reduce.12.cloned.1.call-start = ((), (), s32[]{:S(2)}) async-start(), calls=%async_computation.23 | async-start | bytes 2097152 | tf_op jit(solution)/shard_map/psum | solution.py:170
  795.1 375.8 %reduce-scatter.20.cloned.1.call-start = ((), (), s32[]{:S(2)}) async-start(), calls=%async_computation.22 | async-start | bytes 35651584 | tf_op jit(solution)/shard_map/reduce_scatter | solution.py:271
  812.5 423.4 %reduce-scatter.10.cloned.1.call-start = ((), (), s32[]{:S(2)}) async-start(), calls=%async_computation.17 | async-start | bytes 2228224 | tf_op jit(solution)/shard_map/reduce_scatter | solution.py:266
  815.1 485.8 %reduce-scatter.12.cloned.1.call-start = ((), (), s32[]{:S(2)}) async-start(), calls=%async_computation.18 | async-start | bytes 2228224 | tf_op jit(solution)/shard_map/reduce_scatter | solution.py:267
  817.7 590.2 %reduce-scatter.8.cloned.1.call-start = ((), (), s32[]{:S(2)}) async-start(), calls=%async_computation.16 | async-start | bytes 8912896 | tf_op jit(solution)/shard_map/reduce_scatter | solution.py:265
  823.1 692.4 %reduce-scatter.14.cloned.1.call-start = ((), (), s32[]{:S(2)}) async-start(), calls=%async_computation.19 | async-start | bytes 8912896 | tf_op jit(solution)/shard_map/reduce_scatter | solution.py:268
  828.6 1021.7 %reduce-scatter.16.cloned.1.call-start = ((), (), s32[]{:S(2)}) async-start(), calls=%async_computation.20 | async-start | bytes 35651584 | tf_op jit(solution)/shard_map/reduce_scatter | solution.py:269
  843.1 1341.6 %reduce-scatter.18.cloned.1.call-start = ((), (), s32[]{:S(2)}) async-start(), calls=%async_computation.21 | async-start | bytes 35651584 | tf_op jit(solution)/shard_map/reduce_scatter | solution.py:270
  (11 other events, 92.2 us)
Sparse Core Ops, SparseCore 0:
  10.2 40.5 all-gather.9
  52.9 36.8 all-gather.11
  91.9 49.3 all-gather.13
  143.3 48.8 all-gather.15
  197.1 38.6 all-reduce.7
  237.8 192.3 all-gather.17
  432.4 136.2 all-gather.19
  570.8 124.5 all-gather.21
  733.7 38.2 all-reduce.9
  795.2 40.0 all-reduce.11
  839.6 331.2 reduce-scatter.19
  1175.0 60.8 reduce-scatter.9
  1240.2 60.6 reduce-scatter.11
  1305.4 102.4 reduce-scatter.7
  1412.4 103.0 reduce-scatter.13
  1520.2 330.1 reduce-scatter.15
  1855.0 329.5 reduce-scatter.17
